TPU v7x, 256 devices: a whole 4x4x8 slice. The times are simulated.
256 devices in a mesh: own: 32 (over y, x, core), row: 8 (over z).
Axes of the slice: x: 4, y: 4, z: 8, core: 2. Of those that a mesh axis runs over, the one named last changes fastest.
Arguments:
- weights: float32 [32, 8, 128, 2048], P('own', None, 'row'), may hold values from -200 to 200
- first_moment: float32 [32, 8, 128, 2048], P('own', None, 'row'), may hold values from -20 to 20
- second_moment: float32 [32, 8, 128, 2048], P('own', None, 'row'), may hold values from 0.002 to 0.05
- gradient: bfloat16 [32, 8, 128, 2048], P('own', None, 'row'), may hold values from -0.59765625 to 0.59765625
- owner: int32 [127], replicated, may hold values from 0 to 31, as said below
Outputs:
- new_weights: float32 [32, 8, 128, 2048], P('own', None, 'row')
- new_first: float32 [32, 8, 128, 2048], P('own', None, 'row')
- new_second: float32 [32, 8, 128, 2048], P('own', None, 'row')
- low_weights: bfloat16 [32, 8, 128, 2048], P('own')
- weight_norms: float32 [14], replicated
- update_norms: float32 [14], replicated
- trust_ratios: float32 [14], replicated
Inputs may be any that keep to these rules, and one draw needn't show every extreme that they name: No owner group holds more than 8 tiles, and one holds exactly 8.
All inputs are finite; a program needn't handle non-finite values.
Results may differ from a plain program's by a relative error of at most 0.0004.
Values may be sent and summed in bfloat16 or wider, within the bound.
A program may use at most 128 MiB of HBM per device.

v0:
```python
import jax
import jax.numpy as jnp
import numpy as np
from jax import lax
from jax.sharding import PartitionSpec as P

QW = 4096
KVW = 512
NEXP = 128
FF = 768
EW = 3
TILE = 128
MATS = 14
DECAY = 0.1
STEP_SIZE = 0.05
EPSILON = 1e-06


def matrix_table():
    counts = [QW // TILE, KVW // TILE, KVW // TILE, QW // TILE, NEXP // TILE] + [FF // TILE] * (
        3 * EW
    )
    return np.repeat(np.arange(len(counts)), counts).astype(np.int32)


def slot_select(owner, owners_count, slot_count, matrices):
    tile_table = jnp.asarray(matrix_table())
    owner_hit = (owner[:, None] == jnp.arange(owners_count, dtype=jnp.int32)[None, :]).astype(
        jnp.int32
    )
    tile_rank = jnp.sum((jnp.cumsum(owner_hit, 0) - owner_hit) * owner_hit, 1)
    slot_hit = tile_rank[:, None] == jnp.arange(slot_count, dtype=jnp.int32)[None, :]
    matrix_hit = tile_table[:, None] == jnp.arange(matrices, dtype=jnp.int32)[None, :]
    owner_bool = owner_hit > 0
    joined = (
        owner_bool[:, :, None, None] & slot_hit[:, None, :, None] & matrix_hit[:, None, None, :]
    )
    return jnp.any(joined, axis=0).astype(jnp.float32)


def shards(weights, first_moment, second_moment, gradient, owner):
    slot_count = weights.shape[1]
    select_all = slot_select(owner, lax.axis_size("own"), slot_count, MATS)
    select = lax.dynamic_index_in_dim(select_all, lax.axis_index("own"), 0, keepdims=False)
    used = jnp.sum(select, 1)[None, :, None, None]
    grad_wide = gradient.astype(jnp.float32)
    moment_one = 0.5 * first_moment + 0.5 * grad_wide
    moment_two = 0.5 * second_moment + 0.5 * grad_wide * grad_wide
    direction = moment_one / (jnp.sqrt(moment_two) + EPSILON) + DECAY * weights
    weight_sq = jnp.sum(weights * weights, axis=(2, 3))[0]
    update_sq = jnp.sum(direction * direction, axis=(2, 3))[0]
    weight_part = jnp.sum(select * weight_sq[:, None], 0)
    update_part = jnp.sum(select * update_sq[:, None], 0)
    weight_total, update_total = lax.psum((weight_part, update_part), ("own", "row"))
    weight_norms = jnp.sqrt(weight_total)
    update_norms = jnp.sqrt(update_total)
    trust_ratios = weight_norms / (update_norms + EPSILON)
    slot_ratio = jnp.sum(select * trust_ratios[None, :], 1)[None, :, None, None]
    new_weights = used * (weights - STEP_SIZE * slot_ratio * direction)
    low_weights = lax.all_gather(new_weights.astype(jnp.bfloat16), "row", axis=2, tiled=True)
    new_first = used * moment_one
    new_second = used * moment_two
    return (
        new_weights,
        new_first,
        new_second,
        low_weights,
        weight_norms,
        update_norms,
        trust_ratios,
    )


def solution(mesh):
    placed = (
        P("own", None, "row", None),
        P("own", None, "row", None),
        P("own", None, "row", None),
        P("own", None, "row", None),
        P(),
    )
    return jax.shard_map(
        shards,
        mesh=mesh,
        in_specs=placed,
        out_specs=(
            P("own", None, "row", None),
            P("own", None, "row", None),
            P("own", None, "row", None),
            P("own", None, None, None),
            P(),
            P(),
            P(),
        ),
        check_vma=False,
    )
```

profile of v0, /device:TPU:1, one launch (start us, length us, event | category | flops | bytes accessed | tf_op | source)
XLA Modules:
  0.0 167.5 jit_solution(3595493397532116743)
XLA Ops:
  7.2 0.0 copy-start
  7.2 0.0 all-gather.2.cloned.1.call-start
  7.2 0.7 iota_compare_fusion.1
  8.0 0.7 fusion.4
  8.7 0.1 copy.13
  8.8 0.2 reduce_window_sum.11
  9.0 0.8 select_reduce_fusion
  9.9 7.7 %and_reduce_fusion = pred[32,8,14]{1,2,0:T(8,128)(4,1)S(1)} fusion(pred[127,14]{0,1:T(8,128)(4,1)S(1)} %iota_compare_fusion.1, pred[127,32,8]{0,2,1:T(8,128)(4,1)S(1)} %broadcast_and_fusion), kind=kLoop, calls=%fused_computation | loop fusion | flops 906752 | bytes 37874 | tf_op jit(solution)/shard_map/reduce_or | solution.py:38
  17.7 0.1 copy.14
  17.7 4.3 %multiply_reduce_fusion = (f32[8]{0:T(128)S(1)}, f32[1,8,16,2048]{3,2,1,0:T(8,128)S(1)}, f32[1,8,16,2048]{3,2,1,0:T(8,128)}, f32[1,8,16,2048]{3,2,1,0:T(8,128)}, f32[8]{0:T(128)S(1)}) fusion(f32[1,8,16,2048]{3,2,1,0:T(8,128)} %param.6, f32[1,8,16,2048]{3,2,1,0:T(8,128)} %param.8, bf16[1,8,16,2048]{3,2,1,0:T(8,128)(2,1)} %param.9, ...), kind=kLoop, calls=%fused_computation.5 | loop fusion | flops 4456432 | bytes 6815840 | tf_op jit(solution)/shard_map/reduce_sum | solution.py:51
  22.1 0.1 fusion.6
  22.2 81.4 %all-reduce = (f32[14]{0:T(128)S(1)}, f32[14]{0:T(128)S(1)}) all-reduce(f32[14]{0:T(128)S(1)} %get-tuple-element.8, f32[14]{0:T(128)S(1)} %get-tuple-element.7), channel_id=1, replica_groups=mesh['own'=32,'row'=8] {'own','row'}, use_global_device_ids=true, to_apply=%region_6.7 | all-reduce | flops 28 | bytes 224 | tf_op jit(solution)/shard_map/psum | solution.py:54
  103.6 0.5 add_divide_fusion
  104.1 0.0 copy-start.1
  104.1 0.1 fusion.7
  104.2 0.0 copy-done
  104.2 1.4 fusion.9
  105.6 0.0 all-gather.2.cloned.1.call-update
  105.7 50.2 %all-gather.2.cloned.1.call-done = bf16[1,8,128,2048]{3,2,1,0:T(8,128)(2,1)} async-done(((bf16[1,8,16,2048]{3,2,1,0:T(8,128)(2,1)}), bf16[1,8,128,2048]{3,2,1,0:T(8,128)(2,1)}) %all-gather.2.cloned.1.call-update) | async-done | bytes 4194320 | tf_op jit(solution)/shard_map/all_gather | solution.py:60
  155.8 4.8 %copy.16 = bf16[1,8,128,2048]{3,2,1,0:T(8,128)(2,1)} copy(bf16[1,8,128,2048]{3,2,1,0:T(8,128)(2,1)} %all-gather.2.cloned.1.call-done) | data formatting | bytes 8388608
  160.6 0.0 copy-done.1
  (5 shorter events, 0.1 us)
Async XLA Ops:
  7.2 97.0 %copy-start = (f32[1,8,16,2048]{3,2,1,0:T(8,128)S(1)}, f32[1,8,16,2048]{3,2,1,0:T(8,128)}, u32[]{:S(2)}) copy-start(f32[1,8,16,2048]{3,2,1,0:T(8,128)} %param.6) | copy-start | bytes 3145732
  7.2 148.6 %all-gather.2.cloned.1.call-start = ((), (), s32[]{:S(2)}) async-start(), calls=%async_computation | async-start | bytes 4718592 | tf_op jit(solution)/shard_map/all_gather | solution.py:60
  104.1 56.5 %copy-start.1 = (f32[14]{0:T(128)}, f32[14]{0:T(128)S(1)}, u32[]{:S(2)}) copy-start(f32[14]{0:T(128)S(1)} %get-tuple-element.36) | copy-start | bytes 172
Sparse Core Ops, SparseCore 0:
  105.8 50.0 all-gather.1
where the time goes:
time: 168 us; the launch traced here: 167 us
  blocking collectives  81.4 us (48%)
  waiting for transfers between devices  50.2 us (30%)
  other arithmetic  16.8 us (10%)
  between operations  14.1 us (8%)
  local copies, waits for them, and re-layouts  4.96 us (3%)
    psum x1, blocking collectives, shards(): lax.psum((weight_part, update_part), ('own', 'row'))  81.4 us
    all_gather x1, waiting for transfers between devices, shards(): lax.all_gather(new_weights.astype(jnp.bfloat16), 'row', axis=2, tiled=True)  50.2 us
    reduce_or x1, other arithmetic, slot_select(): return jnp.any(joined, axis=0).astype(jnp.float32)  7.73 us
    unnamed x5, local copies, waits for them, and re-layouts  4.8 us
    reduce_sum x1, other arithmetic, shards(): update_sq = jnp.sum(direction * direction, axis=(2, 3))[0]  4.33 us
  transfers between devices with their start and end apart: 1, of which 1 were waited for; matrix products, arithmetic and copies ran while one was open for 0% of the time, Pallas kernels for 0%

commit v1 on v0

--- a/solution.py
+++ b/solution.py
@@ -57,7 +57,12 @@
     trust_ratios = weight_norms / (update_norms + EPSILON)
     slot_ratio = jnp.sum(select * trust_ratios[None, :], 1)[None, :, None, None]
     new_weights = used * (weights - STEP_SIZE * slot_ratio * direction)
-    low_weights = lax.all_gather(new_weights.astype(jnp.bfloat16), "row", axis=2, tiled=True)
+    low_weights = jnp.concatenate(
+        lax.all_to_all(
+            jnp.stack([new_weights.astype(jnp.bfloat16)] * lax.axis_size("row")), "row", 0, 0
+        ),
+        axis=2,
+    )
     new_first = used * moment_one
     new_second = used * moment_two
     return (

time: 168 us -> 200 us (1.19)
  blocking collectives: 81.4 us -> 180 us
  waiting for transfers between devices: 50.2 us -> 0 us
  between operations: 14.1 us -> 0.71 us
    all_to_all x0 -> x1, blocking collectives: none -> 98.3 us  [shards(): lax.all_to_all(jnp.stack([new_weights.astype(jnp.bfloat16)] * lax.axis_si...]
    all_gather x1 -> x0, waiting for transfers between devices: 50.2 us -> none  [shards(): lax.all_gather(new_weights.astype(jnp.bfloat16), 'row', axis=2, tiled=True)]
    unnamed x5 -> x4, local copies, waits for them, and re-layouts: 4.8 us -> 0.01 us
    all_to_all x0 -> x1, local copies, waits for them, and re-layouts: none -> 2.32 us  [shards(): lax.all_to_all(jnp.stack([new_weights.astype(jnp.bfloat16)] * lax.axis_si...]
  transfers between devices with their start and end apart: 1 -> 0, of which waited for: 1 -> 0; matrix products, arithmetic and copies ran while one was open for 0% -> 0% of each run, Pallas kernels for 0% -> 0%
where the time goes in v1:
time: 200 us
  blocking collectives  180 us (90%)
  other arithmetic  16.6 us (8%)
  local copies, waits for them, and re-layouts  3 us (2%)
    all_to_all x1, blocking collectives, shards(): lax.all_to_all(jnp.stack([new_weights.astype(jnp.bfloat16)] * lax.axis_si...  98.3 us
    psum x1, blocking collectives, shards(): lax.psum((weight_part, update_part), ('own', 'row'))  81.4 us
    reduce_or x1, other arithmetic, slot_select(): return jnp.any(joined, axis=0).astype(jnp.float32)  7.73 us
    reduce_sum x1, other arithmetic, shards(): update_sq = jnp.sum(direction * direction, axis=(2, 3))[0]  4.33 us

profile of v1, /device:TPU:1, one launch (start us, length us, event | category | flops | bytes accessed | tf_op | source)
XLA Modules:
  0.0 200.0 jit_solution(10478098668119659210)
XLA Ops:
  0.6 0.0 copy-start
  0.6 0.8 iota_compare_fusion.1
  1.4 0.7 fusion.4
  2.1 0.1 copy.14
  2.2 0.2 reduce_window_sum.11
  2.4 0.8 select_reduce_fusion
  3.3 7.7 %and_reduce_fusion = pred[32,8,14]{1,2,0:T(8,128)(4,1)S(1)} fusion(pred[127,14]{0,1:T(8,128)(4,1)S(1)} %iota_compare_fusion.1, pred[127,32,8]{0,2,1:T(8,128)(4,1)S(1)} %broadcast_and_fusion), kind=kLoop, calls=%fused_computation | loop fusion | flops 906752 | bytes 37874 | tf_op jit(solution)/shard_map/reduce_or | solution.py:38
  11.1 0.1 copy.15
  11.2 4.3 %multiply_reduce_fusion = (f32[8]{0:T(128)S(1)}, f32[1,8,16,2048]{3,2,1,0:T(8,128)S(1)}, f32[1,8,16,2048]{3,2,1,0:T(8,128)}, f32[1,8,16,2048]{3,2,1,0:T(8,128)}, f32[8]{0:T(128)S(1)}) fusion(f32[1,8,16,2048]{3,2,1,0:T(8,128)} %param.6, f32[1,8,16,2048]{3,2,1,0:T(8,128)} %param.8, bf16[1,8,16,2048]{3,2,1,0:T(8,128)(2,1)} %param.9, ...), kind=kLoop, calls=%fused_computation.5 | loop fusion | flops 4456432 | bytes 6815840 | tf_op jit(solution)/shard_map/reduce_sum | solution.py:51
  15.5 0.1 fusion.6
  15.6 81.4 %all-reduce = (f32[14]{0:T(128)S(1)}, f32[14]{0:T(128)S(1)}) all-reduce(f32[14]{0:T(128)S(1)} %get-tuple-element.8, f32[14]{0:T(128)S(1)} %get-tuple-element.7), channel_id=1, replica_groups=mesh['own'=32,'row'=8] {'own','row'}, use_global_device_ids=true, to_apply=%region_6.7 | all-reduce | flops 28 | bytes 224 | tf_op jit(solution)/shard_map/psum | solution.py:54
  97.0 0.5 add_divide_fusion
  97.5 0.0 copy-start.1
  97.5 0.1 fusion.7
  97.6 0.0 copy-done
  97.6 1.2 convert_bitcast_fusion
  98.9 0.5 stack.2
  99.4 0.0 copy-done.1
  99.4 98.3 %all_to_all.5 = bf16[8,1,8,16,2048]{4,3,2,1,0:T(8,128)(2,1)S(1)} all-to-all(bf16[8,1,8,16,2048]{4,3,2,1,0:T(8,128)(2,1)S(1)} %stack.2), channel_id=1, replica_groups=mesh['own'=32,'row'=8] {'row'}, dimensions={0} | all-to-all | bytes 8388608 | tf_op jit(solution)/shard_map/all_to_all | solution.py:61
  197.7 2.3 %copy.16 = bf16[8,1,8,16,2048]{4,3,0,2,1:T(8,128)(2,1)} copy(bf16[8,1,8,16,2048]{4,3,2,1,0:T(8,128)(2,1)S(1)} %all_to_all.5) | data formatting | bytes 8388608 | tf_op jit(solution)/shard_map/all_to_all | solution.py:61
  (5 shorter events, 0.1 us)
Async XLA Ops:
  0.6 97.0 %copy-start = (f32[1,8,16,2048]{3,2,1,0:T(8,128)S(1)}, f32[1,8,16,2048]{3,2,1,0:T(8,128)}, u32[]{:S(2)}) copy-start(f32[1,8,16,2048]{3,2,1,0:T(8,128)} %param.6) | copy-start | bytes 3145732
  97.5 1.9 copy-start.1
